TPU v7x, 32 devices: a whole 2x2x4 slice. The times are simulated.
32 devices in a mesh: dp: 8 (over y, x, core), tensor: 4 (over z).
Axes of the slice: x: 2, y: 2, z: 4, core: 2. Of those that a mesh axis runs over, the one named last changes fastest.
Arguments:
- tokens: bfloat16 [16384, 768], P(('dp', 'tensor')), may hold values from -6 to 6
- starts: int32 [8, 8], P('dp'), may hold values from 0 to 2047, as said below
- w_qkv: bfloat16 [768, 2304], P(None, 'tensor'), may hold values from -0.21875 to 0.21875
- b_qkv: bfloat16 [2304], P('tensor'), may hold values from -3 to 3
- w_out: bfloat16 [768, 768], P('tensor'), may hold values from -2 to 2
- b_out: bfloat16 [768], replicated, may hold values from -3 to 3
- gain_one: bfloat16 [768], replicated, may hold values from 0.099609375 to 1.8984375
- shift_one: bfloat16 [768], replicated, may hold values from -3 to 3
- w_in: bfloat16 [768, 3072], P(None, 'tensor'), may hold values from -0.21875 to 0.21875
- b_in: bfloat16 [3072], P('tensor'), may hold values from -3 to 3
- w_two: bfloat16 [3072, 768], P('tensor'), may hold values from -0.21875 to 0.21875
- b_two: bfloat16 [768], replicated, may hold values from -3 to 3
- gain_two: bfloat16 [768], replicated, may hold values from 0.099609375 to 1.8984375
- shift_two: bfloat16 [768], replicated, may hold values from -3 to 3
- cotangent: bfloat16 [16384, 768], P(('dp', 'tensor')), may hold values from -6 to 6
Outputs:
- block_out: bfloat16 [16384, 768], P(('dp', 'tensor'))
- d_tokens: bfloat16 [16384, 768], P(('dp', 'tensor'))
- d_w_qkv: float32 [768, 2304], P(None, 'tensor')
- d_b_qkv: float32 [2304], P('tensor')
- d_w_out: float32 [768, 768], P('tensor')
- d_b_out: float32 [768], replicated
- d_gain_one: float32 [768], replicated
- d_shift_one: float32 [768], replicated
- d_w_in: float32 [768, 3072], P(None, 'tensor')
- d_b_in: float32 [3072], P('tensor')
- d_w_two: float32 [3072, 768], P('tensor')
- d_b_two: float32 [768], replicated
- d_gain_two: float32 [768], replicated
- d_shift_two: float32 [768], replicated
Inputs may be any that keep to these rules, and one draw needn't show every extreme that they name: Each row holds exactly 8 documents: its first start is 0 and its starts rise strictly. In the first row the last document is a single token.
All inputs are finite; a program needn't handle non-finite values.
Results may differ from a plain program's by a relative error of at most 0.014.
Values may be sent and summed in bfloat16 or wider, within the bound.
No kernel may reach another device: no remote copies, remote signals or barrier semaphores. Data moves between devices by JAX's collectives and lax.ppermute only.
A program may use at most 192 MiB of HBM per device.

v0:
```python
import math
import jax
import jax.numpy as jnp
from jax import lax
from jax.sharding import PartitionSpec as P

HEAD = 64
GROUP = 64
ROW_LEN = 2048
DOCS = 8
highest = lax.Precision.HIGHEST


def doc_tables(starts_row):
    places = jnp.arange(ROW_LEN, dtype=jnp.int32)
    started = (places[:, None] >= starts_row[None, :]).astype(jnp.int32)
    doc_ids = jnp.sum(started, axis=1) - 1
    onehot = (doc_ids[:, None] == jnp.arange(DOCS, dtype=jnp.int32)[None, :]).astype(jnp.int32)
    finish = jnp.concatenate([starts_row[1:], jnp.full((1,), ROW_LEN, jnp.int32)])
    own_start = jnp.sum(onehot * starts_row[None, :], axis=1)
    own_len = jnp.sum(onehot * (finish - starts_row)[None, :], axis=1)
    angles = 0.5 * math.pi * (places - own_start).astype(jnp.float32) / own_len.astype(jnp.float32)
    return (angles, doc_ids)


def attend(mixed, angles, doc_ids):
    length = mixed.shape[0]
    head_count = mixed.shape[1] // (3 * HEAD)
    blocks = length // GROUP
    pieces = mixed.reshape(blocks, GROUP, head_count, 3, HEAD)
    queries = jax.nn.relu(pieces[:, :, :, 0])
    key_pos = jax.nn.relu(pieces[:, :, :, 1])
    values = pieces[:, :, :, 2]
    cosine = jnp.cos(angles).reshape(blocks, GROUP, 1, 1)
    sines = jnp.sin(angles).reshape(blocks, GROUP, 1, 1)
    query_feat = jnp.concatenate([queries * cosine, queries * sines], axis=-1)
    key_feat = jnp.concatenate([key_pos * cosine, key_pos * sines], axis=-1)
    doc_blocks = doc_ids.reshape(blocks, GROUP)
    within = jnp.arange(GROUP, dtype=jnp.int32)
    inside_mask = (
        (doc_blocks[:, :, None] == doc_blocks[:, None, :])
        & (within[None, :, None] >= within[None, None, :])
    ).astype(jnp.float32)
    scores = (
        jnp.einsum("bihf,bjhf->bhij", query_feat, key_feat, precision=highest)
        * inside_mask[:, None]
    )
    numerator = jnp.einsum("bhij,bjhd->bihd", scores, values, precision=highest)
    denominator = jnp.transpose(jnp.sum(scores, axis=-1), (0, 2, 1))
    first_doc = doc_blocks[:, 0]
    last_doc = doc_blocks[:, -1]
    tail_mask = (doc_blocks == last_doc[:, None]).astype(jnp.float32)
    states = jnp.einsum("bjhf,bjhd,bj->bhfd", key_feat, values, tail_mask, precision=highest)
    key_sums = jnp.einsum("bjhf,bj->bhf", key_feat, tail_mask, precision=highest)
    order = jnp.arange(blocks, dtype=jnp.int32)
    link_mask = (
        (last_doc[None, :] == first_doc[:, None]) & (order[None, :] < order[:, None])
    ).astype(jnp.float32)
    carried = jnp.einsum("cb,bhfd->chfd", link_mask, states, precision=highest)
    carried_sum = jnp.einsum("cb,bhf->chf", link_mask, key_sums, precision=highest)
    opening = (doc_blocks == first_doc[:, None]).astype(jnp.float32)
    numerator = numerator + jnp.einsum(
        "bihf,bhfd,bi->bihd", query_feat, carried, opening, precision=highest
    )
    denominator = denominator + jnp.einsum(
        "bihf,bhf,bi->bih", query_feat, carried_sum, opening, precision=highest
    )
    result = numerator / jnp.maximum(denominator, 1.0)[..., None]
    return result.reshape(length, head_count * HEAD)


def attend_rows(mixed, angles, doc_ids):
    row_count = angles.shape[0]
    shaped = mixed.reshape(row_count, angles.shape[1], mixed.shape[1])
    return jax.vmap(attend)(shaped, angles, doc_ids).reshape(mixed.shape[0], -1)


def normalize(rows_in, gain, shift):
    centred = rows_in - jnp.mean(rows_in, axis=-1, keepdims=True)
    spread = jnp.mean(centred * centred, axis=-1, keepdims=True)
    return centred * lax.rsqrt(spread + 1e-05) * gain + shift


def smooth(values):
    return jax.nn.gelu(values)


def inner_rows(left, right):
    return lax.dot_general(
        left, right, (((0,), (0,)), ((), ())), preferred_element_type=jnp.float32
    )


def times_rows(left, right):
    return lax.dot_general(
        left, right, (((1,), (1,)), ((), ())), preferred_element_type=jnp.float32
    )


def rows_product(source, weight):
    return jnp.dot(source, weight, preferred_element_type=jnp.float32)


def rows_back(source, weight):
    return times_rows(source, weight)


def on_device(
    tokens,
    starts,
    w_qkv,
    b_qkv,
    w_out,
    b_out,
    gain_one,
    shift_one,
    w_in,
    b_in,
    w_two,
    b_two,
    gain_two,
    shift_two,
    cotangent,
):
    angles, doc_ids = jax.vmap(doc_tables)(starts)
    bias_qkv = b_qkv.astype(jnp.float32)
    bias_in = b_in.astype(jnp.float32)
    gain_a = gain_one.astype(jnp.float32)
    shift_a = shift_one.astype(jnp.float32)
    gain_b = gain_two.astype(jnp.float32)
    shift_b = shift_two.astype(jnp.float32)
    input_full = lax.all_gather(tokens, "tensor", axis=0, tiled=True)
    mixed = jnp.dot(input_full, w_qkv, preferred_element_type=jnp.float32) + bias_qkv
    attended = attend_rows(mixed, angles, doc_ids).astype(jnp.bfloat16)
    branch = lax.psum_scatter(
        rows_product(attended, w_out), "tensor", scatter_dimension=0, tiled=True
    ) + b_out.astype(jnp.float32)
    first_sum = tokens.astype(jnp.float32) + branch
    first_low = normalize(first_sum, gain_a, shift_a).astype(jnp.bfloat16)
    middle_full = lax.all_gather(first_low, "tensor", axis=0, tiled=True)
    hidden = jnp.dot(middle_full, w_in, preferred_element_type=jnp.float32) + bias_in
    active = smooth(hidden).astype(jnp.bfloat16)
    second = lax.psum_scatter(
        rows_product(active, w_two), "tensor", scatter_dimension=0, tiled=True
    ) + b_two.astype(jnp.float32)
    second_sum = first_low.astype(jnp.float32) + second
    block_out = normalize(second_sum, gain_b, shift_b).astype(jnp.bfloat16)
    input_back = lax.all_gather(tokens, "tensor", axis=0, tiled=True)
    middle_back = lax.all_gather(first_low, "tensor", axis=0, tiled=True)
    unused_two, norm_two_back = jax.vjp(normalize, second_sum, gain_b, shift_b)
    d_r2, d_gain_two, d_shift_two = norm_two_back(cotangent.astype(jnp.float32))
    d_second = d_r2.astype(jnp.bfloat16)
    d_b_two = jnp.sum(d_second, axis=0, dtype=jnp.float32)
    second_full = lax.all_gather(d_second, "tensor", axis=0, tiled=True)
    hidden_again = jnp.dot(middle_back, w_in, preferred_element_type=jnp.float32) + bias_in
    active_val, gelu_back = jax.vjp(smooth, hidden_again)
    active_again = active_val.astype(jnp.bfloat16)
    d_w_two = inner_rows(active_again, second_full)
    d_active = times_rows(second_full, w_two)
    d_hidden = gelu_back(d_active)[0].astype(jnp.bfloat16)
    d_b_in = jnp.sum(d_hidden, axis=0, dtype=jnp.float32)
    d_w_in = inner_rows(middle_back, d_hidden)
    d_first = (
        lax.psum_scatter(rows_back(d_hidden, w_in), "tensor", scatter_dimension=0, tiled=True)
        + d_r2
    )
    unused_one, norm_one_back = jax.vjp(normalize, first_sum, gain_a, shift_a)
    d_r1, d_gain_one, d_shift_one = norm_one_back(d_first)
    d_branch = d_r1.astype(jnp.bfloat16)
    d_b_out = jnp.sum(d_branch, axis=0, dtype=jnp.float32)
    branch_full = lax.all_gather(d_branch, "tensor", axis=0, tiled=True)
    mixed_again = jnp.dot(input_back, w_qkv, preferred_element_type=jnp.float32) + bias_qkv
    attended_val, attend_back = jax.vjp(
        lambda mixed_in: attend_rows(mixed_in, angles, doc_ids), mixed_again
    )
    attended_again = attended_val.astype(jnp.bfloat16)
    d_w_out = inner_rows(attended_again, branch_full)
    d_attended = times_rows(branch_full, w_out)
    d_mixed = attend_back(d_attended)[0].astype(jnp.bfloat16)
    d_b_qkv = jnp.sum(d_mixed, axis=0, dtype=jnp.float32)
    d_w_qkv = inner_rows(input_back, d_mixed)
    d_tokens = (
        lax.psum_scatter(
            rows_back(d_mixed, w_qkv).astype(jnp.bfloat16),
            "tensor",
            scatter_dimension=0,
            tiled=True,
        ).astype(jnp.float32)
        + d_r1
    ).astype(jnp.bfloat16)
    d_w_qkv, d_b_qkv, d_w_out, d_w_in, d_b_in, d_w_two = lax.psum(
        (d_w_qkv, d_b_qkv, d_w_out, d_w_in, d_b_in, d_w_two), "dp"
    )
    d_b_out, d_gain_one, d_shift_one, d_b_two, d_gain_two, d_shift_two = lax.psum(
        (d_b_out, d_gain_one, d_shift_one, d_b_two, d_gain_two, d_shift_two), ("dp", "tensor")
    )
    return (
        block_out,
        d_tokens,
        d_w_qkv,
        d_b_qkv,
        d_w_out,
        d_b_out,
        d_gain_one,
        d_shift_one,
        d_w_in,
        d_b_in,
        d_w_two,
        d_b_two,
        d_gain_two,
        d_shift_two,
    )


def solution(mesh):
    in_specs = (
        P(("dp", "tensor"), None),
        P("dp", None),
        P(None, "tensor"),
        P("tensor"),
        P("tensor", None),
        P(),
        P(),
        P(),
        P(None, "tensor"),
        P("tensor"),
        P("tensor", None),
        P(),
        P(),
        P(),
        P(("dp", "tensor"), None),
    )
    out_specs = (
        P(("dp", "tensor"), None),
        P(("dp", "tensor"), None),
        P(None, "tensor"),
        P("tensor"),
        P("tensor", None),
        P(),
        P(),
        P(),
        P(None, "tensor"),
        P("tensor"),
        P("tensor", None),
        P(),
        P(),
        P(),
    )
    return jax.shard_map(
        on_device, mesh=mesh, in_specs=in_specs, out_specs=out_specs, check_vma=False
    )
```

profile of v0, /device:TPU:0, one launch (start us, length us, event | category | flops | bytes accessed | tf_op | source)
XLA Modules:
  0.0 1038.7 jit_solution(10530214980209661449)
XLA Ops:
  12.7 63.1 %all-gather.5.cloned.1.call-done = bf16[2048,768]{1,0:T(8,128)(2,1)} async-done(((bf16[512,768]{1,0:T(8,128)(2,1)}), bf16[2048,768]{1,0:T(8,128)(2,1)}) %all-gather.5.cloned.1.call-update) | async-done | bytes 3145744 | tf_op jit(solution)/shard_map/all_gather | solution.py:132
  82.2 8.7 reshape_reshape.3
  90.9 8.2 fusion.101
  150.5 9.1 divide_convert_fusion
  169.7 107.1 %reduce-scatter.5.cloned.1.call-done = f32[512,768]{1,0:T(8,128)} async-done(((f32[2048,768]{1,0:T(8,128)}), f32[512,768]{1,0:T(8,128)}) %reduce-scatter.5.cloned.1.call-update) | async-done | bytes 1572880 | tf_op jit(solution)/shard_map/reduce_scatter | solution.py:135
  280.2 64.1 %all-gather.7.cloned.1.call-done = bf16[2048,768]{1,0:T(8,128)(2,1)} async-done(((bf16[512,768]{1,0:T(8,128)(2,1)}), bf16[2048,768]{1,0:T(8,128)(2,1)}) %all-gather.7.cloned.1.call-update) | async-done | bytes 3145744 | tf_op jit(solution)/shard_map/all_gather | solution.py:140
  344.3 8.4 multiply_convert_fusion
  361.3 107.1 %reduce-scatter.7.cloned.1.call-done = f32[512,768]{1,0:T(8,128)} async-done(((f32[2048,768]{1,0:T(8,128)}), f32[512,768]{1,0:T(8,128)}) %reduce-scatter.7.cloned.1.call-update) | async-done | bytes 1572880 | tf_op jit(solution)/shard_map/reduce_scatter | solution.py:143
  476.5 64.1 %all-gather.9.cloned.1.call-done = bf16[2048,768]{1,0:T(8,128)(2,1)} async-done(((bf16[512,768]{1,0:T(8,128)(2,1)}), bf16[2048,768]{1,0:T(8,128)(2,1)}) %all-gather.9.cloned.1.call-update) | async-done | bytes 3145744 | tf_op jit(solution)/shard_map/all_gather | solution.py:154
  540.6 9.8 convert_reduce_fusion.1
  556.7 109.5 %reduce-scatter.9.cloned.1.call-done = f32[512,768]{1,0:T(8,128)} async-done(((f32[2048,768]{1,0:T(8,128)}), f32[512,768]{1,0:T(8,128)}) %reduce-scatter.9.cloned.1.call-update) | async-done | bytes 1572880 | tf_op jit(solution)/shard_map/reduce_scatter | solution.py:164
  673.7 63.5 %all-gather.11.cloned.1.call-done = bf16[2048,768]{1,0:T(8,128)(2,1)} async-done(((bf16[512,768]{1,0:T(8,128)(2,1)}), bf16[2048,768]{1,0:T(8,128)(2,1)}) %all-gather.11.cloned.1.call-update) | async-done | bytes 3145744 | tf_op jit(solution)/shard_map/all_gather | solution.py:171
  742.9 12.0 %fusion.21 = f32[32,3,64,64]{2,3,1,0:T(8,128)} fusion(f32[32,3,64,64]{2,3,1,0:T(8,128)} %copy-done.21, f32[32,64,64]{1,2,0:T(8,128)S(1)} %copy-done.12, f32[1,32,64,3,64]{2,1,4,3,0:T(8,128)} %reshape.798, f32[32,64,3]{1,2,0:T(4,128)S(1)} %copy-done.42), kind=kOutput, calls=%fused_computation.38 | convolution fusion | flops 302776320 | bytes 5267456 | tf_op jit(solution)/shard_map/transpose(jvp(vmap(bhij,bjhd->bihd)))/dot_general | solution.py:48
  754.9 7.4 fusion.19
  777.2 8.3 fusion.42
  795.2 7.7 fusion.13
  802.9 7.0 fusion.38
  814.7 8.1 add_bitcast_fusion
  828.5 7.4 copy.171
  835.9 6.7 convert_element_type.170
  847.0 7.1 fusion.108
  864.5 43.0 %all-reduce.3 = (f32[768]{0:T(1024)}, f32[768]{0:T(1024)}, f32[768]{0:T(1024)}, f32[768]{0:T(1024)}, f32[768]{0:T(1024)}, /*index=5*/f32[768]{0:T(1024)}) all-reduce(f32[768]{0:T(1024)S(1)} %copy-done.71, f32[768]{0:T(1024)S(1)} %copy-done.72, f32[768]{0:T(1024)S(1)} %copy-done.73, ...), channel_id=1, replica_groups=mesh['dp'=8,'tensor'=4] {'dp','tensor'}, use_global_device_ids=true, to_apply=%region_22.23 | all-reduce | flops 4608 | bytes 36864 | tf_op jit(solution)/shard_map/psum | solution.py:194
  907.5 14.0 %all-reduce.4 = (f32[576]{0:T(1024)}, f32[768]{0:T(1024)}) all-reduce(f32[576]{0:T(1024)S(1)} %reduce_sum.223, f32[768]{0:T(1024)S(1)} %copy-done.76), channel_id=1, replica_groups=mesh['dp'=8,'tensor'=4] {'dp'}, use_global_device_ids=true, to_apply=%region_19.20 | all-reduce | flops 1344 | bytes 10752 | tf_op jit(solution)/shard_map/psum | solution.py:191
  923.8 101.3 %all-reduce.8.cloned.1.call-done = (f32[768,576]{0,1:T(8,128)}, f32[192,768]{1,0:T(8,128)}, f32[768,768]{1,0:T(8,128)}, f32[768,768]{1,0:T(8,128)}) async-done(((f32[768,576]{0,1:T(8,128)}, f32[192,768]{1,0:T(8,128)}, f32[768,768]{1,0:T(8,128)}, f32[768,768]{1,0:T(8,128)}), (f32[768,576]{0,1:T(8,128)}, f32[192,768]{1,0:T(8,128)}, f32[768,768]{1,0:T(8,128)}, ...) | async-done | bytes 7077904 | tf_op jit(solution)/shard_map/psum | solution.py:191
  (289 shorter events, 170.7 us)
Async XLA Ops:
  7.2 337.2 %copy-start = (bf16[768,768]{1,0:T(8,128)(2,1)S(1)}, bf16[768,768]{1,0:T(8,128)(2,1)}, u32[]{:S(2)}) copy-start(bf16[768,768]{1,0:T(8,128)(2,1)} %param.23) | copy-start | bytes 3538948
  7.2 68.6 %all-gather.5.cloned.1.call-start = ((), (), s32[]{:S(2)}) async-start(), calls=%async_computation.4 | async-start | bytes 3932160 | tf_op jit(solution)/shard_map/all_gather | solution.py:132
  7.9 268.9 %reduce-scatter.5.cloned.1.call-start = ((), (), s32[]{:S(2)}) async-start(), calls=%async_computation.5 | async-start | bytes 7864320 | tf_op jit(solution)/shard_map/reduce_scatter | solution.py:135
  12.1 117.7 %copy-start.61 = (s32[32]{0:T(128)}, s32[32]{0:T(128)S(1)}, u32[]{:S(2)}) copy-start(s32[32]{0:T(128)S(1)} %get-tuple-element.20) | copy-start | bytes 388
  12.1 117.7 %copy-start.64 = (s32[32]{0:T(128)}, s32[32]{0:T(128)S(1)}, u32[]{:S(2)}) copy-start(s32[32]{0:T(128)S(1)} %get-tuple-element.21) | copy-start | bytes 388
  12.2 109.0 %copy-start.39 = (f32[32,64]{1,0:T(8,128)}, f32[32,64]{1,0:T(8,128)S(1)}, u32[]{:S(2)}) copy-start(f32[32,64]{1,0:T(8,128)S(1)} %get-tuple-element.57) | copy-start | bytes 24580
  12.3 98.5 %copy-start.44 = (f32[32,64]{1,0:T(8,128)}, f32[32,64]{1,0:T(8,128)S(1)}, u32[]{:S(2)}) copy-start(f32[32,64]{1,0:T(8,128)S(1)} %get-tuple-element.71) | copy-start | bytes 24580
  12.3 98.4 %copy-start.46 = (f32[32,64]{1,0:T(8,128)}, f32[32,64]{1,0:T(8,128)S(1)}, u32[]{:S(2)}) copy-start(f32[32,64]{1,0:T(8,128)S(1)} %get-tuple-element.72) | copy-start | bytes 24580
  12.7 131.7 %copy-start.11 = (f32[32,64,64]{1,2,0:T(8,128)}, f32[32,64,64]{1,2,0:T(8,128)S(1)}, u32[]{:S(2)}) copy-start(f32[32,64,64]{1,2,0:T(8,128)S(1)} %and_convert_fusion) | copy-start | bytes 1572868
  167.2 109.6 %copy-start.27 = (bf16[512,768]{1,0:T(8,128)(2,1)S(1)}, bf16[512,768]{1,0:T(8,128)(2,1)}, u32[]{:S(2)}) copy-start(bf16[512,768]{1,0:T(8,128)(2,1)} %param.15) | copy-start | bytes 2359300
  167.3 177.1 %all-gather.7.cloned.1.call-start = ((), (), s32[]{:S(2)}) async-start(), calls=%async_computation.6 | async-start | bytes 3932160 | tf_op jit(solution)/shard_map/all_gather | solution.py:140
  278.6 74.1 %copy-start.50 = (f32[512]{0:T(512)}, f32[512]{0:T(512)S(1)}, u32[]{:S(2)}) copy-start(f32[512]{0:T(512)S(1)} %broadcast_multiply_fusion.1) | copy-start | bytes 6148
  278.9 73.8 %copy-start.57 = (f32[512]{0:T(512)}, f32[512]{0:T(512)S(1)}, u32[]{:S(2)}) copy-start(f32[512]{0:T(512)S(1)} %multiply_reduce_fusion.5) | copy-start | bytes 6148
  280.2 188.3 %reduce-scatter.7.cloned.1.call-start = ((), (), s32[]{:S(2)}) async-start(), calls=%async_computation.7 | async-start | bytes 7864320 | tf_op jit(solution)/shard_map/reduce_scatter | solution.py:143
  358.9 181.8 %all-gather.9.cloned.1.call-start = ((), (), s32[]{:S(2)}) async-start(), calls=%async_computation.8 | async-start | bytes 3932160 | tf_op jit(solution)/shard_map/all_gather | solution.py:154
  361.3 109.5 %copy-start.26 = (bf16[512,768]{1,0:T(8,128)(2,1)S(1)}, bf16[512,768]{1,0:T(8,128)(2,1)}, u32[]{:S(2)}) copy-start(bf16[512,768]{1,0:T(8,128)(2,1)} %param.29) | copy-start | bytes 2359300
  476.4 189.7 %reduce-scatter.9.cloned.1.call-start = ((), (), s32[]{:S(2)}) async-start(), calls=%async_computation.9 | async-start | bytes 7864320 | tf_op jit(solution)/shard_map/reduce_scatter | solution.py:164
  556.6 109.6 %copy-start.49 = (f32[768]{0:T(1024)S(1)}, f32[768]{0:T(1024)}, u32[]{:S(2)}) copy-start(f32[768]{0:T(1024)} %convert_element_type.155) | copy-start | bytes 9220
  556.6 109.6 %copy-start.51 = (f32[512]{0:T(512)S(1)}, f32[512]{0:T(512)}, u32[]{:S(2)}) copy-start(f32[512]{0:T(512)} %copy-done.50) | copy-start | bytes 6148
  556.6 109.6 %copy-start.54 = (f32[512]{0:T(512)S(1)}, f32[512]{0:T(512)}, u32[]{:S(2)}) copy-start(f32[512]{0:T(512)} %copy-done.53) | copy-start | bytes 6148
  556.6 112.9 %copy-start.58 = (f32[512]{0:T(512)S(1)}, f32[512]{0:T(512)}, u32[]{:S(2)}) copy-start(f32[512]{0:T(512)} %copy-done.57) | copy-start | bytes 6148
  556.6 180.5 %all-gather.11.cloned.1.call-start = ((), (), s32[]{:S(2)}) async-start(), calls=%async_computation.10 | async-start | bytes 3932160 | tf_op jit(solution)/shard_map/all_gather | solution.py:171
  673.0 248.5 %reduce-scatter.11.cloned.1.call-start = ((), (), s32[]{:S(2)}) async-start(), calls=%async_computation.11 | async-start | bytes 3932160 | tf_op jit(solution)/shard_map/reduce_scatter | solution.py:183
  846.7 178.4 %all-reduce.8.cloned.1.call-start = ((), (), s32[]{:S(2)}) async-start(), calls=%async_computation.12 | async-start | bytes 14155776 | tf_op jit(solution)/shard_map/psum | solution.py:191
  (76 other events, 865.4 us)
Sparse Core Ops, SparseCore 0:
  9.6 66.1 all-gather.4
  167.4 109.3 reduce-scatter.4
  280.3 64.0 all-gather.6
  359.0 109.3 reduce-scatter.6
  476.6 64.0 all-gather.8
  556.7 109.3 reduce-scatter.8
  673.1 64.0 all-gather.10
  846.8 59.8 reduce-scatter.10
  911.5 113.5 all-reduce.7
where the time goes:
time: 1050 us; the launch traced here: 1040 us
  waiting for transfers between devices  681 us (65%)
  matrix products  166 us (16%)
  local copies, waits for them, and re-layouts  73.7 us (7%)
  blocking collectives  57 us (5%)
  other arithmetic  45.5 us (4%)
  between operations  15.3 us (1%)
    reduce_scatter x1, waiting for transfers between devices, on_device(): lax.psum_scatter(rows_back(d_hidden, w_in), 'tensor', scatter_dimension=0...  109 us
    reduce_scatter x1, waiting for transfers between devices, on_device(): lax.psum_scatter(rows_product(attended, w_out), 'tensor', scatter_dimensi...  107 us
    reduce_scatter x1, waiting for transfers between devices, on_device(): lax.psum_scatter(rows_product(active, w_two), 'tensor', scatter_dimension...  107 us
    psum x1, waiting for transfers between devices, on_device(): lax.psum((d_w_qkv, d_b_qkv, d_w_out, d_w_in, d_b_in, d_w_two), 'dp')  101 us
    all_gather x1, waiting for transfers between devices, on_device(): second_full = lax.all_gather(d_second, 'tensor', axis=0, tiled=True)  64.1 us
    all_gather x1, waiting for transfers between devices, on_device(): middle_full = lax.all_gather(first_low, 'tensor', axis=0, tiled=True)  64.1 us
    all_gather x1, waiting for transfers between devices, on_device(): branch_full = lax.all_gather(d_branch, 'tensor', axis=0, tiled=True)  63.5 us
    all_gather x1, waiting for transfers between devices, on_device(): input_full = lax.all_gather(tokens, 'tensor', axis=0, tiled=True)  63.1 us
  transfers between devices with their start and end apart: 9, of which 8 were waited for; matrix products, arithmetic and copies ran while one was open for 3% of the time, Pallas kernels for 0%

commit v1 on v0

--- a/solution.py
+++ b/solution.py
@@ -137,7 +137,15 @@
     ) + b_out.astype(jnp.float32)
     first_sum = tokens.astype(jnp.float32) + branch
     first_low = normalize(first_sum, gain_a, shift_a).astype(jnp.bfloat16)
-    middle_full = lax.all_gather(first_low, "tensor", axis=0, tiled=True)
+    ways, here, step = (lax.axis_size("tensor"), lax.axis_index("tensor"), first_low.shape[0])
+    line, have = (first_low, 1)
+    while have < ways:
+        line = jnp.concatenate(
+            [line, lax.ppermute(line, "tensor", [(d, (d - have) % ways) for d in range(ways)])],
+            axis=0,
+        )
+        have = 2 * have
+    middle_full = jnp.roll(line, here * step, axis=0)
     hidden = jnp.dot(middle_full, w_in, preferred_element_type=jnp.float32) + bias_in
     active = smooth(hidden).astype(jnp.bfloat16)
     second = lax.psum_scatter(

time: 1050 us -> 1140 us (1.086)
  waiting for transfers between devices: 681 us -> 745 us
    ppermute x0 -> x2, waiting for transfers between devices: none -> 81.2 us  [on_device(): lax.ppermute(line, 'tensor', [(d, (d - have) % ways) for d in range(ways)])]
  transfers between devices with their start and end apart: 9 -> 11, of which waited for: 8 -> 10; matrix products, arithmetic and copies ran while one was open for 3% -> 4% of each run, Pallas kernels for 0% -> 0%
where the time goes in v1:
time: 1140 us; the launch traced here: 1130 us
  waiting for transfers between devices  745 us (65%)
  matrix products  173 us (15%)
  local copies, waits for them, and re-layouts  82.6 us (7%)
  blocking collectives  57.9 us (5%)
  other arithmetic  49.9 us (4%)
  between operations  15.3 us (1%)
    reduce_scatter x1, waiting for transfers between devices, on_device(): lax.psum_scatter(rows_back(d_hidden, w_in), 'tensor', scatter_dimension=0...  109 us
    reduce_scatter x1, waiting for transfers between devices, on_device(): lax.psum_scatter(rows_product(active, w_two), 'tensor', scatter_dimension...  107 us
    reduce_scatter x1, waiting for transfers between devices, on_device(): lax.psum_scatter(rows_product(attended, w_out), 'tensor', scatter_dimensi...  107 us
    psum x1, waiting for transfers between devices, on_device(): lax.psum((d_w_qkv, d_b_qkv, d_w_out, d_w_in, d_b_in, d_w_two), 'dp')  96.9 us
    ppermute x2, waiting for transfers between devices, on_device(): lax.ppermute(line, 'tensor', [(d, (d - have) % ways) for d in range(ways)])  81.2 us
    all_gather x1, waiting for transfers between devices, on_device(): branch_full = lax.all_gather(d_branch, 'tensor', axis=0, tiled=True)  63.5 us
    all_gather x1, waiting for transfers between devices, on_device(): input_full = lax.all_gather(tokens, 'tensor', axis=0, tiled=True)  63.1 us
    all_gather x1, waiting for transfers between devices, on_device(): middle_back = lax.all_gather(first_low, 'tensor', axis=0, tiled=True)  58.2 us
  transfers between devices with their start and end apart: 11, of which 10 were waited for; matrix products, arithmetic and copies ran while one was open for 4% of the time, Pallas kernels for 0%

profile of v1, /device:TPU:0, one launch (start us, length us, event | category | flops | bytes accessed | tf_op | source)
XLA Modules:
  0.0 1130.4 jit_solution(855860276207121101)
XLA Ops:
  12.7 63.1 %all-gather.5.cloned.1.call-done = bf16[2048,768]{1,0:T(8,128)(2,1)} async-done(((bf16[512,768]{1,0:T(8,128)(2,1)}), bf16[2048,768]{1,0:T(8,128)(2,1)}) %all-gather.5.cloned.1.call-update) | async-done | bytes 3145744 | tf_op jit(solution)/shard_map/all_gather | solution.py:132
  82.2 8.7 reshape_reshape.3
  90.9 8.1 fusion.124
  150.5 9.1 divide_convert_fusion
  169.7 107.1 %reduce-scatter.5.cloned.1.call-done = f32[512,768]{1,0:T(8,128)} async-done(((f32[2048,768]{1,0:T(8,128)}), f32[512,768]{1,0:T(8,128)}) %reduce-scatter.5.cloned.1.call-update) | async-done | bytes 1572880 | tf_op jit(solution)/shard_map/reduce_scatter | solution.py:135
  283.3 17.0 %collective-permute-done = bf16[512,768]{1,0:T(8,128)(2,1)S(1)} collective-permute-done((bf16[512,768]{1,0:T(8,128)(2,1)S(1)}, bf16[512,768]{1,0:T(8,128)(2,1)S(1)}, u32[]{:S(2)}, u32[]{:S(2)}) %collective-permute-start) | collective-permute-done | bytes 786464 | tf_op jit(solution)/shard_map/ppermute | solution.py:144
  308.6 64.2 %collective-permute-done.1 = bf16[1024,768]{1,0:T(8,128)(2,1)} collective-permute-done((bf16[1024,768]{1,0:T(8,128)(2,1)}, bf16[1024,768]{1,0:T(8,128)(2,1)}, u32[]{:S(2)}, u32[]{:S(2)}) %collective-permute-start.1) | collective-permute-done | bytes 1572896 | tf_op jit(solution)/shard_map/ppermute | solution.py:144
  380.2 9.4 fusion.79
  394.0 107.5 %reduce-scatter.7.cloned.1.call-done = f32[512,768]{1,0:T(8,128)} async-done(((f32[2048,768]{1,0:T(8,128)}), f32[512,768]{1,0:T(8,128)}) %reduce-scatter.7.cloned.1.call-update) | async-done | bytes 1572880 | tf_op jit(solution)/shard_map/reduce_scatter | solution.py:151
  509.4 58.2 %all-gather.9.cloned.1.call-done = bf16[2048,768]{1,0:T(8,128)(2,1)} async-done(((bf16[512,768]{1,0:T(8,128)(2,1)}), bf16[2048,768]{1,0:T(8,128)(2,1)}) %all-gather.9.cloned.1.call-update) | async-done | bytes 3145744 | tf_op jit(solution)/shard_map/all_gather | solution.py:157
  574.7 57.0 %all-gather.7.cloned.1.call-done = bf16[2048,768]{1,0:T(8,128)(2,1)} async-done(((bf16[512,768]{1,0:T(8,128)(2,1)}), bf16[2048,768]{1,0:T(8,128)(2,1)}) %all-gather.7.cloned.1.call-update) | async-done | bytes 3145744 | tf_op jit(solution)/shard_map/all_gather | solution.py:162
  631.7 9.8 convert_reduce_fusion.1
  647.8 109.5 %reduce-scatter.9.cloned.1.call-done = f32[512,768]{1,0:T(8,128)} async-done(((f32[2048,768]{1,0:T(8,128)}), f32[512,768]{1,0:T(8,128)}) %reduce-scatter.9.cloned.1.call-update) | async-done | bytes 1572880 | tf_op jit(solution)/shard_map/reduce_scatter | solution.py:172
  764.9 63.5 %all-gather.11.cloned.1.call-done = bf16[2048,768]{1,0:T(8,128)(2,1)} async-done(((bf16[512,768]{1,0:T(8,128)(2,1)}), bf16[2048,768]{1,0:T(8,128)(2,1)}) %all-gather.11.cloned.1.call-update) | async-done | bytes 3145744 | tf_op jit(solution)/shard_map/all_gather | solution.py:179
  834.1 12.0 %fusion.29 = f32[32,3,64,64]{2,3,1,0:T(8,128)} fusion(f32[32,3,64,64]{2,3,1,0:T(8,128)} %copy-done.23, f32[32,64,64]{1,2,0:T(8,128)S(1)} %copy-done.12, f32[1,32,64,3,64]{2,1,4,3,0:T(8,128)} %reshape.798, f32[32,64,3]{1,2,0:T(4,128)S(1)} %copy-done.46), kind=kOutput, calls=%fused_computation.47 | convolution fusion | flops 302776320 | bytes 5267456 | tf_op jit(solution)/shard_map/transpose(jvp(vmap(bhij,bjhd->bihd)))/dot_general | solution.py:48
  846.1 7.4 fusion.27
  868.4 8.3 fusion.52
  886.4 7.7 fusion.21
  906.0 8.1 add_bitcast_fusion
  919.8 7.4 copy.171
  945.6 7.9 fusion.39
  959.6 43.6 %all-reduce.3 = (f32[768]{0:T(1024)}, f32[768]{0:T(1024)}, f32[768]{0:T(1024)}, f32[768]{0:T(1024)}, f32[768]{0:T(1024)}, /*index=5*/f32[768]{0:T(1024)}) all-reduce(f32[768]{0:T(1024)S(1)} %copy-done.75, f32[768]{0:T(1024)S(1)} %copy-done.76, f32[768]{0:T(1024)S(1)} %copy-done.77, ...), channel_id=1, replica_groups=mesh['dp'=8,'tensor'=4] {'dp','tensor'}, use_global_device_ids=true, to_apply=%region_22.23 | all-reduce | flops 4608 | bytes 36864 | tf_op jit(solution)/shard_map/psum | solution.py:202
  1003.3 14.3 %all-reduce.4 = (f32[576]{0:T(1024)}, f32[768]{0:T(1024)}) all-reduce(f32[576]{0:T(1024)S(1)} %reduce_sum.223, f32[768]{0:T(1024)S(1)} %copy-done.81), channel_id=1, replica_groups=mesh['dp'=8,'tensor'=4] {'dp'}, use_global_device_ids=true, to_apply=%region_19.20 | all-reduce | flops 1344 | bytes 10752 | tf_op jit(solution)/shard_map/psum | solution.py:199
  1019.9 96.9 %all-reduce.8.cloned.1.call-done = (f32[768,576]{0,1:T(8,128)}, f32[192,768]{1,0:T(8,128)}, f32[768,768]{1,0:T(8,128)}, f32[768,768]{1,0:T(8,128)}) async-done(((f32[768,576]{0,1:T(8,128)}, f32[192,768]{1,0:T(8,128)}, f32[768,768]{1,0:T(8,128)}, f32[768,768]{1,0:T(8,128)}), (f32[768,576]{0,1:T(8,128)}, f32[192,768]{1,0:T(8,128)}, f32[768,768]{1,0:T(8,128)}, ...) | async-done | bytes 7077904 | tf_op jit(solution)/shard_map/psum | solution.py:199
  (295 shorter events, 209.2 us)
Async XLA Ops:
  7.2 373.0 %copy-start = (bf16[768,768]{1,0:T(8,128)(2,1)S(1)}, bf16[768,768]{1,0:T(8,128)(2,1)}, u32[]{:S(2)}) copy-start(bf16[768,768]{1,0:T(8,128)(2,1)} %param.23) | copy-start | bytes 3538948
  7.2 68.6 %all-gather.5.cloned.1.call-start = ((), (), s32[]{:S(2)}) async-start(), calls=%async_computation.4 | async-start | bytes 3932160 | tf_op jit(solution)/shard_map/all_gather | solution.py:132
  7.9 268.9 %reduce-scatter.5.cloned.1.call-start = ((), (), s32[]{:S(2)}) async-start(), calls=%async_computation.5 | async-start | bytes 7864320 | tf_op jit(solution)/shard_map/reduce_scatter | solution.py:135
  12.1 117.6 %copy-start.64 = (s32[32]{0:T(128)}, s32[32]{0:T(128)S(1)}, u32[]{:S(2)}) copy-start(s32[32]{0:T(128)S(1)} %get-tuple-element.20) | copy-start | bytes 388
  12.1 117.6 %copy-start.67 = (s32[32]{0:T(128)}, s32[32]{0:T(128)S(1)}, u32[]{:S(2)}) copy-start(s32[32]{0:T(128)S(1)} %get-tuple-element.21) | copy-start | bytes 388
  12.2 108.9 %copy-start.43 = (f32[32,64]{1,0:T(8,128)}, f32[32,64]{1,0:T(8,128)S(1)}, u32[]{:S(2)}) copy-start(f32[32,64]{1,0:T(8,128)S(1)} %get-tuple-element.59) | copy-start | bytes 24580
  12.3 98.4 %copy-start.48 = (f32[32,64]{1,0:T(8,128)}, f32[32,64]{1,0:T(8,128)S(1)}, u32[]{:S(2)}) copy-start(f32[32,64]{1,0:T(8,128)S(1)} %get-tuple-element.73) | copy-start | bytes 24580
  12.7 131.6 %copy-start.11 = (f32[32,64,64]{1,2,0:T(8,128)}, f32[32,64,64]{1,2,0:T(8,128)S(1)}, u32[]{:S(2)}) copy-start(f32[32,64,64]{1,2,0:T(8,128)S(1)} %and_convert_fusion) | copy-start | bytes 1572868
  167.2 109.6 %copy-start.31 = (bf16[512,768]{1,0:T(8,128)(2,1)S(1)}, bf16[512,768]{1,0:T(8,128)(2,1)}, u32[]{:S(2)}) copy-start(bf16[512,768]{1,0:T(8,128)(2,1)} %param.15) | copy-start | bytes 2359300
  167.2 334.3 %reduce-scatter.7.cloned.1.call-start = ((), (), s32[]{:S(2)}) async-start(), calls=%async_computation.6 | async-start | bytes 7864320 | tf_op jit(solution)/shard_map/reduce_scatter | solution.py:151
  280.7 19.6 %collective-permute-start = (bf16[512,768]{1,0:T(8,128)(2,1)S(1)}, bf16[512,768]{1,0:T(8,128)(2,1)S(1)}, u32[]{:S(2)}, u32[]{:S(2)}) collective-permute-start(bf16[512,768]{1,0:T(8,128)(2,1)S(1)} %get-tuple-element.56), channel_id=1, source_target_pairs={{0,3},{1,0},{2,1},{3,2},{4,7},{5,4},{6,5},{7,6},{8,11},{9,8},{10,9... | collective-permute-start | bytes 2359304 | tf_op jit(solution)/shard_map/ppermute | solution.py:144
  302.4 70.4 %collective-permute-start.1 = (bf16[1024,768]{1,0:T(8,128)(2,1)}, bf16[1024,768]{1,0:T(8,128)(2,1)}, u32[]{:S(2)}, u32[]{:S(2)}) collective-permute-start(bf16[1024,768]{1,0:T(8,128)(2,1)} %pad_maximum_fusion), channel_id=1, source_target_pairs={{0,2},{1,3},{2,0},{3,1},{4,6},{5,7},{6,4},{7,5},{8,10},{9,11},{10,... | collective-permute-start | bytes 4718600 | tf_op jit(solution)/shard_map/ppermute | solution.py:144
  389.5 112.0 %copy-start.15 = (bf16[512,768]{1,0:T(8,128)(2,1)S(1)}, bf16[512,768]{1,0:T(8,128)(2,1)}, u32[]{:S(2)}) copy-start(bf16[512,768]{1,0:T(8,128)(2,1)} %copy-done.14) | copy-start | bytes 2359300
  389.6 178.0 %all-gather.9.cloned.1.call-start = ((), (), s32[]{:S(2)}) async-start(), calls=%async_computation.8 | async-start | bytes 3932160 | tf_op jit(solution)/shard_map/all_gather | solution.py:157
  390.2 241.6 %all-gather.7.cloned.1.call-start = ((), (), s32[]{:S(2)}) async-start(), calls=%async_computation.7 | async-start | bytes 3932160 | tf_op jit(solution)/shard_map/all_gather | solution.py:162
  509.3 122.4 %copy-start.79 = (f32[768]{0:T(1024)S(1)}, f32[768]{0:T(1024)}, u32[]{:S(2)}) copy-start(f32[768]{0:T(1024)} %convert_element_type.161) | copy-start | bytes 9220
  509.3 248.0 %reduce-scatter.9.cloned.1.call-start = ((), (), s32[]{:S(2)}) async-start(), calls=%async_computation.9 | async-start | bytes 7864320 | tf_op jit(solution)/shard_map/reduce_scatter | solution.py:172
  647.7 109.6 %copy-start.54 = (f32[768]{0:T(1024)S(1)}, f32[768]{0:T(1024)}, u32[]{:S(2)}) copy-start(f32[768]{0:T(1024)} %convert_element_type.157) | copy-start | bytes 9220
  647.7 109.6 %copy-start.56 = (f32[512]{0:T(512)S(1)}, f32[512]{0:T(512)}, u32[]{:S(2)}) copy-start(f32[512]{0:T(512)} %copy-done.55) | copy-start | bytes 6148
  647.7 109.6 %copy-start.59 = (f32[512]{0:T(512)S(1)}, f32[512]{0:T(512)}, u32[]{:S(2)}) copy-start(f32[512]{0:T(512)} %copy-done.58) | copy-start | bytes 6148
  647.7 112.9 %copy-start.61 = (f32[512]{0:T(512)S(1)}, f32[512]{0:T(512)}, u32[]{:S(2)}) copy-start(f32[512]{0:T(512)} %copy-done.60) | copy-start | bytes 6148
  647.7 180.6 %all-gather.11.cloned.1.call-start = ((), (), s32[]{:S(2)}) async-start(), calls=%async_computation.10 | async-start | bytes 3932160 | tf_op jit(solution)/shard_map/all_gather | solution.py:179
  764.1 253.5 %reduce-scatter.11.cloned.1.call-start = ((), (), s32[]{:S(2)}) async-start(), calls=%async_computation.11 | async-start | bytes 3932160 | tf_op jit(solution)/shard_map/reduce_scatter | solution.py:191
  938.2 178.6 %all-reduce.8.cloned.1.call-start = ((), (), s32[]{:S(2)}) async-start(), calls=%async_computation.12 | async-start | bytes 14155776 | tf_op jit(solution)/shard_map/psum | solution.py:199
  (76 other events, 922.1 us)
Sparse Core Ops, SparseCore 0:
  9.6 66.1 all-gather.4
  167.4 109.3 reduce-scatter.4
  389.7 111.7 reduce-scatter.6
  503.5 64.0 all-gather.8
  569.5 62.1 all-gather.6
  647.8 109.3 reduce-scatter.8
  764.3 64.0 all-gather.10
  938.3 59.9 reduce-scatter.10
  1003.1 113.6 all-reduce.7
